TPU v7x, 256 devices: a whole 4x4x8 slice. The times are simulated.
256 devices in a mesh: op: 16 (over y, z_hi), right: 16 (over z_lo, x, core).
Axes of the slice: x: 4, y: 4, z: 8 (z_hi: 4, z_lo: 2; z = z_hi * 2 + z_lo), core: 2. Of those that a mesh axis runs over, the one named last changes fastest.
Arguments:
- psi: float32 [768, 16384], P('op', 'right'), may hold values from -6 to 6
- left_env: float32 [32, 768, 768], P('op', 'right'), may hold values from -0.078125 to 0.078125
- right_env: float32 [32, 16384, 1024], P('op', 'right'), may hold values from -0.1875 to 0.1875
- sector_lengths: int32 [4], replicated, may hold values from 128 to 384, as said below
- op_map: int32 [32, 4], replicated, may hold values from 0 to 3
Outputs:
- h_psi: float32 [768, 16384], P('op', 'right')
Inputs may be any that keep to these rules, and one draw needn't show every extreme that they name: `sector_lengths`: one sector, at a position that varies between draws, holds 384 states; every other sector holds 128.
All inputs are finite; a program needn't handle non-finite values.
Results may differ from a plain program's by a relative error of at most 0.0003.
Values sent between devices are 32-bit elements; how exact they have to be, the bound alone decides.
A program may use at most 64 MiB of HBM per device.

v0:
```python
import jax
import jax.numpy as jnp
from jax import lax
from jax.sharding import PartitionSpec as P


def on_device(psi, left_env, right_env, sector_lengths, op_map):
    terms = left_env.shape[0]
    width = left_env.shape[2]
    ends = jnp.cumsum(sector_lengths)
    places = jnp.arange(width, dtype=jnp.int32)
    sector = jnp.sum((places[:, None] >= ends[None, :]).astype(jnp.int32), axis=1)
    local_map = lax.dynamic_slice_in_dim(op_map, lax.axis_index("op") * terms, terms, 0)
    count = sector_lengths.shape[0]
    onehot = (sector[:, None] == jnp.arange(count, dtype=jnp.int32)[None, :]).astype(jnp.int32)
    targets = jnp.sum(onehot[None, :, :] * local_map[:, None, :], axis=2)
    whole = lax.all_gather(psi, "op", axis=0, tiled=True)
    inner = jnp.einsum("ac,wbc->wab", whole, right_env, precision=lax.Precision.HIGHEST)
    keep = (sector[None, :, None] == targets[:, None, :]).astype(jnp.float32)
    masked = lax.all_gather(left_env, "right", axis=1, tiled=True) * keep
    summed = jnp.einsum("wra,wab->rb", masked, inner, precision=lax.Precision.HIGHEST)
    return lax.psum_scatter(summed, "op", scatter_dimension=0, tiled=True)


def solution(mesh):
    in_specs = (P("op", "right"), P("op", "right", None), P("op", "right", None), P(), P())
    out_specs = P("op", "right")
    return jax.shard_map(
        on_device, mesh=mesh, in_specs=in_specs, out_specs=out_specs, check_vma=False
    )
```

profile of v0, /device:TPU:2, one launch (start us, length us, event | category | flops | bytes accessed | tf_op | source)
XLA Modules:
  0.0 239.5 jit_solution(2700261651093496640)
XLA Ops:
  6.5 0.0 copy-start
  6.5 0.0 all-gather.5.cloned.1.call-start
  6.5 0.7 all-gather.5.cloned.1.call-update
  7.3 0.0 all-gather.3.cloned.1.call-start
  7.3 0.7 all-gather.3.cloned.1.call-update
  8.0 0.0 reduce-scatter.2.cloned.1.call-start
  8.1 0.8 reduce-window.8
  8.9 0.0 copy-done
  8.9 0.1 constant_dynamic-slice_fusion
  9.0 0.1 copy.7
  9.1 0.1 convert_reduce_fusion
  9.2 0.1 multiply_reduce_fusion
  9.2 71.2 %all-gather.5.cloned.1.call-done = f32[768,1024]{1,0:T(8,128)} async-done(((f32[48,1024]{1,0:T(8,128)}), f32[768,1024]{1,0:T(8,128)}) %all-gather.5.cloned.1.call-update) | async-done | bytes 3145744 | tf_op jit(solution)/shard_map/all_gather | solution.py:17
  80.5 24.4 %fusion.4 = f32[2,1024,768]{1,2,0:T(8,128)} fusion(f32[2,1024,1024]{2,1,0:T(8,128)} %param.7, f32[768,1024]{1,0:T(8,128)} %all-gather.5.cloned.1.call-done), kind=kOutput, calls=%fused_computation.4 | convolution fusion | flops 19327352832 | bytes 17825792 | tf_op jit(solution)/shard_map/ac,wbc->wab/dot_general | solution.py:18
  104.8 16.0 %all-gather.3.cloned.1.call-done = f32[2,768,768]{2,1,0:T(8,128)} async-done(((f32[2,48,768]{2,1,0:T(8,128)}), f32[2,768,768]{2,1,0:T(8,128)}) %all-gather.3.cloned.1.call-update) | async-done | bytes 4718608 | tf_op jit(solution)/shard_map/all_gather | solution.py:20
  120.9 19.9 %fusion.9 = f32[768,1024]{1,0:T(8,128)} fusion(f32[2,1024,768]{1,2,0:T(8,128)} %fusion.4, f32[2,768,768]{2,1,0:T(8,128)} %all-gather.3.cloned.1.call-done, s32[2,768]{1,0:T(2,128)S(1)} %multiply_reduce_fusion, s32[768]{0:T(1024)S(1)} %convert_reduce_fusion), kind=kOutput, calls=%fused_computation.9 | convolution fusion | flops 14497873920 | bytes 14164992 | tf_op jit(solution)/shard_map/wra,wab->rb/dot_general | solution.py:21
  140.7 0.0 reduce-scatter.2.cloned.1.call-update
  140.8 92.2 %reduce-scatter.2.cloned.1.call-done = f32[48,1024]{1,0:T(8,128)} async-done(((f32[768,1024]{1,0:T(8,128)}), f32[48,1024]{1,0:T(8,128)}) %reduce-scatter.2.cloned.1.call-update) | async-done | bytes 196624 | tf_op jit(solution)/shard_map/reduce_scatter | solution.py:22
  (1 shorter events, 0.0 us)
Async XLA Ops:
  6.5 2.4 copy-start
  6.5 73.9 %all-gather.5.cloned.1.call-start = ((), (), s32[]{:S(2)}) async-start(), calls=%async_computation.2 | async-start | bytes 3342336 | tf_op jit(solution)/shard_map/all_gather | solution.py:17
  7.3 113.6 %all-gather.3.cloned.1.call-start = ((), (), s32[]{:S(2)}) async-start(), calls=%async_computation.1 | async-start | bytes 5013504 | tf_op jit(solution)/shard_map/all_gather | solution.py:20
  8.0 224.9 %reduce-scatter.2.cloned.1.call-start = ((), (), s32[]{:S(2)}) async-start(), calls=%async_computation.3 | async-start | bytes 3342336 | tf_op jit(solution)/shard_map/reduce_scatter | solution.py:22
Sparse Core Ops, SparseCore 0:
  9.8 70.5 all-gather.4
  82.3 38.5 all-gather.2
  140.9 92.0 reduce-scatter.1
where the time goes:
time: 240 us; the launch traced here: 239 us
  waiting for transfers between devices  181 us (75%)
  matrix products  44.3 us (18%)
  between operations  13.1 us (5%)
    reduce_scatter x1, waiting for transfers between devices, on_device(): return lax.psum_scatter(summed, 'op', scatter_dimension=0, tiled=True)  92.2 us
    all_gather x1, waiting for transfers between devices, on_device(): whole = lax.all_gather(psi, 'op', axis=0, tiled=True)  71.2 us
    dot_general x1, matrix products, on_device(): jnp.einsum('ac,wbc->wab', whole, right_env, precision=lax.Precision.HIGHEST)  24.4 us
    dot_general x1, matrix products, on_device(): jnp.einsum('wra,wab->rb', masked, inner, precision=lax.Precision.HIGHEST)  19.9 us
    all_gather x1, waiting for transfers between devices, on_device(): masked = lax.all_gather(left_env, 'right', axis=1, tiled=True) * keep  16 us
  transfers between devices with their start and end apart: 3, of which 3 were waited for; matrix products, arithmetic and copies ran while one was open for 11% of the time, Pallas kernels for 0%

commit v1 on v0

--- a/solution.py
+++ b/solution.py
@@ -14,7 +14,10 @@
     count = sector_lengths.shape[0]
     onehot = (sector[:, None] == jnp.arange(count, dtype=jnp.int32)[None, :]).astype(jnp.int32)
     targets = jnp.sum(onehot[None, :, :] * local_map[:, None, :], axis=2)
-    whole = lax.all_gather(psi, "op", axis=0, tiled=True)
+    size = lax.axis_size("op")
+    shards = jnp.stack([psi for _ in range(size)])
+    shards = lax.all_to_all(shards, "op", split_axis=0, concat_axis=0)
+    whole = jnp.concatenate(shards, axis=0)
     inner = jnp.einsum("ac,wbc->wab", whole, right_env, precision=lax.Precision.HIGHEST)
     keep = (sector[None, :, None] == targets[:, None, :]).astype(jnp.float32)
     masked = lax.all_gather(left_env, "right", axis=1, tiled=True) * keep

time: 240 us -> 256 us (1.067)
  starting transfers between devices: 0.08 us -> 11.2 us
  waiting for transfers between devices: 181 us -> 184 us
  local copies, waits for them, and re-layouts: 0.17 us -> 3.16 us
    all_to_all x0 -> x1, waiting for transfers between devices: none -> 75.4 us  [on_device(): shards = lax.all_to_all(shards, 'op', split_axis=0, concat_axis=0)]
    all_gather x1 -> x0, waiting for transfers between devices: 71.2 us -> none  [on_device(): whole = lax.all_gather(psi, 'op', axis=0, tiled=True)]
    all_gather x1, waiting for transfers between devices: 16 us -> 0.01 us  [on_device(): masked = lax.all_gather(left_env, 'right', axis=1, tiled=True) * keep]
    reduce_scatter x1, waiting for transfers between devices: 92.2 us -> 108 us  [on_device(): return lax.psum_scatter(summed, 'op', scatter_dimension=0, tiled=True)]
    all_to_all x0 -> x1, starting transfers between devices: none -> 11.2 us  [on_device(): shards = lax.all_to_all(shards, 'op', split_axis=0, concat_axis=0)]
    another operation x0 -> x1, local copies, waits for them, and re-layouts: none -> 2.99 us  [on_device(): shards = jnp.stack([psi for _ in range(size)])]
  transfers between devices with their start and end apart: 3 -> 3, of which waited for: 3 -> 2; matrix products, arithmetic and copies ran while one was open for 11% -> 11% of each run, Pallas kernels for 0% -> 0%
where the time goes in v1:
time: 256 us
  waiting for transfers between devices  184 us (72%)
  matrix products  44 us (17%)
  between operations  13.4 us (5%)
  starting transfers between devices  11.2 us (4%)
  local copies, waits for them, and re-layouts  3.16 us (1%)
    reduce_scatter x1, waiting for transfers between devices, on_device(): return lax.psum_scatter(summed, 'op', scatter_dimension=0, tiled=True)  108 us
    all_to_all x1, waiting for transfers between devices, on_device(): shards = lax.all_to_all(shards, 'op', split_axis=0, concat_axis=0)  75.4 us
    dot_general x1, matrix products, on_device(): jnp.einsum('ac,wbc->wab', whole, right_env, precision=lax.Precision.HIGHEST)  24.1 us
    dot_general x1, matrix products, on_device(): jnp.einsum('wra,wab->rb', masked, inner, precision=lax.Precision.HIGHEST)  19.9 us
    all_to_all x1, starting transfers between devices, on_device(): shards = lax.all_to_all(shards, 'op', split_axis=0, concat_axis=0)  11.2 us
  transfers between devices with their start and end apart: 3, of which 2 were waited for; matrix products, arithmetic and copies ran while one was open for 11% of the time, Pallas kernels for 0%

profile of v1, /device:TPU:2, one launch (start us, length us, event | category | flops | bytes accessed | tf_op | source)
XLA Modules:
  0.0 255.9 jit_solution(10345859354932936538)
XLA Ops:
  6.5 0.0 copy-start
  6.5 0.0 all-gather.2.cloned.1.call-start
  6.5 0.7 all-gather.2.cloned.1.call-update
  7.3 0.0 copy-start.1
  7.3 3.0 %stack.2 = f32[16,48,1024]{2,1,0:T(8,128)} broadcast(f32[48,1024]{1,0:T(8,128)} %param.5), dimensions={1,2} | broadcast | bytes 3342336 | tf_op jit(solution)/shard_map/stack | solution.py:18
  10.3 11.2 %all-to-all-start = ((f32[16,48,1024]{2,1,0:T(8,128)}), f32[16,48,1024]{2,1,0:T(8,128)S(1)}, u32[]{:S(2)}, u32[]{:S(2)}) async-start(f32[16,48,1024]{2,1,0:T(8,128)} %stack.2), calls=%async_computation | async-start | bytes 6291456 | tf_op jit(solution)/shard_map/all_to_all | solution.py:19
  21.5 0.0 reduce-scatter.2.cloned.1.call-start
  21.5 0.0 copy-done.1
  21.5 0.2 reduce-window.8
  21.7 0.0 copy-done
  21.7 0.1 constant_dynamic-slice_fusion
  21.8 0.1 copy.7
  21.9 0.1 convert_reduce_fusion
  22.0 0.1 multiply_reduce_fusion
  22.1 75.4 %all-to-all-done = f32[16,48,1024]{2,1,0:T(8,128)S(1)} async-done(((f32[16,48,1024]{2,1,0:T(8,128)}), f32[16,48,1024]{2,1,0:T(8,128)S(1)}, u32[]{:S(2)}, u32[]{:S(2)}) %all-to-all-start) | async-done | bytes 3145760 | tf_op jit(solution)/shard_map/all_to_all | solution.py:19
  97.4 24.1 %fusion.14 = f32[2,1024,768]{1,2,0:T(8,128)} fusion(f32[2,1024,1024]{2,1,0:T(8,128)} %param.7, f32[768,1024,1]{1,0,2:T(8,128)S(1)} %bitcast.14), kind=kOutput, calls=%fused_computation.15 | convolution fusion | flops 19327352832 | bytes 17825792 | tf_op jit(solution)/shard_map/ac,wbc->wab/dot_general | solution.py:21
  121.6 0.0 all-gather.2.cloned.1.call-done
  121.6 19.9 %fusion.7 = f32[768,1024]{1,0:T(8,128)} fusion(f32[2,1024,768]{1,2,0:T(8,128)} %fusion.14, f32[2,768,768]{2,1,0:T(8,128)} %all-gather.2.cloned.1.call-done, s32[2,768]{1,0:T(2,128)S(1)} %multiply_reduce_fusion, s32[768]{0:T(1024)S(1)} %convert_reduce_fusion), kind=kOutput, calls=%fused_computation.7 | convolution fusion | flops 14497873920 | bytes 14164992 | tf_op jit(solution)/shard_map/wra,wab->rb/dot_general | solution.py:24
  141.5 0.0 reduce-scatter.2.cloned.1.call-update
  141.5 107.6 %reduce-scatter.2.cloned.1.call-done = f32[48,1024]{1,0:T(8,128)} async-done(((f32[768,1024]{1,0:T(8,128)}), f32[48,1024]{1,0:T(8,128)}) %reduce-scatter.2.cloned.1.call-update) | async-done | bytes 196624 | tf_op jit(solution)/shard_map/reduce_scatter | solution.py:25
  (1 shorter events, 0.0 us)
Async XLA Ops:
  6.5 15.2 %copy-start = (s32[32,4]{0,1:T(4,128)S(1)}, s32[32,4]{0,1:T(4,128)}, u32[]{:S(2)}) copy-start(s32[32,4]{0,1:T(4,128)} %param.9) | copy-start | bytes 1540
  6.5 115.0 %all-gather.2.cloned.1.call-start = ((), (), s32[]{:S(2)}) async-start(), calls=%async_computation.2 | async-start | bytes 5013504 | tf_op jit(solution)/shard_map/all_gather | solution.py:23
  7.3 14.3 %copy-start.1 = (s32[4]{0:T(128)S(1)}, s32[4]{0:T(128)}, u32[]{:S(2)}) copy-start(s32[4]{0:T(128)} %param.8) | copy-start | bytes 52
  10.3 87.2 %all-to-all-start = ((f32[16,48,1024]{2,1,0:T(8,128)}), f32[16,48,1024]{2,1,0:T(8,128)S(1)}, u32[]{:S(2)}, u32[]{:S(2)}) async-start(f32[16,48,1024]{2,1,0:T(8,128)} %stack.2), calls=%async_computation | async-start | bytes 6291456 | tf_op jit(solution)/shard_map/all_to_all | solution.py:19
  21.5 227.6 %reduce-scatter.2.cloned.1.call-start = ((), (), s32[]{:S(2)}) async-start(), calls=%async_computation.3 | async-start | bytes 3342336 | tf_op jit(solution)/shard_map/reduce_scatter | solution.py:25
Sparse Core Ops, SparseCore 0:
  9.2 87.3 all-gather.1
  141.6 107.4 reduce-scatter.1
